TPU v7x, 512 devices: a whole 4x4x16 slice. The times are simulated.
512 devices in a mesh: field: 32 (over z_hi, x, core), point: 16 (over y, z_lo).
Axes of the slice: x: 4, y: 4, z: 16 (z_hi: 4, z_lo: 4; z = z_hi * 4 + z_lo), core: 2. Of those that a mesh axis runs over, the one named last changes fastest.
Arguments:
- residual_in: bfloat16 [32, 4096, 2048], P('field', 'point'), may hold values from -6 to 6
- coefs_in: bfloat16 [32, 4096, 4, 256], P('field', 'point'), may hold values from 0 to 1
- dictionary: bfloat16 [8192, 2048], P('field'), may hold values from -0.125 to 0.125
- owner_order: int32 [32], replicated, may hold values from 0 to 31, each once
- pixel_of: int32 [32, 4096], P('field', 'point'), may hold values from 0 to 4095, each once within a row
Outputs:
- maps: float32 [32, 4, 256, 32, 128], P('field', None, 'point')
Inputs may be any that keep to these rules, and one draw needn't show every extreme that they name: `owner_order`: A permutation of the dictionary blocks. `pixel_of`: each field's row is a permutation of its scan points over the 32 x 128 pixels.
All inputs are finite; a program needn't handle non-finite values.
Results may differ from a plain program's by a relative error of at most 0.00045.
Values may be sent and summed in bfloat16 or wider, within the bound.
A program may use at most 64 MiB of HBM per device.

v0:
```python
import jax
import jax.numpy as jnp
from jax import lax
from jax.sharding import PartitionSpec as P

TURNS = 4
SWEEPS = 4
MAP_W = 128
time_step = 0.2
edge_scale = 0.5


def from_root(value, axis, source):
    kept = jnp.where(lax.axis_index(axis) == source, value, 0).astype(value.dtype)
    return lax.psum(kept, axis)


def block_steps(templates):
    gram = lax.dot_general(
        templates, templates, (((1,), (1,)), ((), ())), preferred_element_type=jnp.float32
    )
    return 1.0 / jnp.sum(jnp.abs(gram), axis=1)


def diffuse(grids):
    for repeat in range(SWEEPS):
        padded = jnp.pad(grids, ((0, 0), (1, 1), (1, 1)), mode="edge")
        summed = jnp.zeros_like(grids)
        for neighbour in (
            padded[:, :-2, 1:-1],
            padded[:, 2:, 1:-1],
            padded[:, 1:-1, :-2],
            padded[:, 1:-1, 2:],
        ):
            differ = neighbour - grids
            scaled = differ / edge_scale
            summed = summed + differ / (1.0 + scaled * scaled)
        grids = grids + time_step * summed
    return grids


def build_maps(moved, pixel_ids):
    points = moved.shape[0]
    count = moved.shape[1]
    local_kb = moved.shape[2]
    values = moved.reshape(points, count * local_kb).T
    flat = jnp.zeros((count * local_kb, points), jnp.float32).at[:, pixel_ids].set(values)
    grids = diffuse(flat.reshape(count * local_kb, points // MAP_W, MAP_W))
    return grids.reshape(count, local_kb, points // MAP_W, MAP_W)


def per_device(residual_in, coefs_in, dictionary, owner_order, pixel_of):
    residual = residual_in[0]
    coefs = coefs_in[0].astype(jnp.float32)
    pixel_ids = lax.all_gather(pixel_of[0], "point", axis=0, tiled=True)
    updated = []
    for turn_index in range(TURNS):
        owner = owner_order[turn_index]
        templates = from_root(dictionary, "field", owner)
        step_size = block_steps(templates)
        correlation = lax.dot_general(
            residual, templates, (((1,), (1,)), ((), ())), preferred_element_type=jnp.float32
        )
        before = coefs[:, turn_index, :]
        after = jnp.maximum(before + step_size[None, :] * correlation, 0.0)
        updated.append(after)
        if turn_index + 1 < TURNS:
            change = (after - before).astype(jnp.bfloat16)
            residual = (
                residual.astype(jnp.float32)
                - jnp.dot(change, templates, preferred_element_type=jnp.float32)
            ).astype(jnp.bfloat16)
    stacked = jnp.stack(updated, axis=1)
    maps = build_maps(
        lax.all_to_all(stacked, "point", split_axis=2, concat_axis=0, tiled=True), pixel_ids
    )
    return maps[None]


def solution(mesh):
    placed = (
        P("field", "point", None),
        P("field", "point", None, None),
        P("field", None),
        P(),
        P("field", "point"),
    )
    return jax.shard_map(
        per_device,
        mesh=mesh,
        in_specs=placed,
        out_specs=P("field", None, "point", None, None),
        check_vma=False,
    )
```

profile of v0, /device:TPU:32, one launch (start us, length us, event | category | flops | bytes accessed | tf_op | source)
XLA Modules:
  0.0 503.0 jit_solution(4180003535699886071)
XLA Ops:
  6.5 0.0 all-reduce.3.cloned.1.call-start
  6.5 1.5 fusion.46
  10.5 3.3 broadcast_select_fusion.3
  13.8 0.0 copy-start.4
  13.9 0.0 all-reduce.3.cloned.1.call-update
  13.9 1.0 copy-done.4
  14.9 0.3 copy.27
  15.2 0.1 bitcast_convert_fusion
  15.3 0.0 copy-start
  15.3 382.6 %all-reduce.3.cloned.1.call-done = (bf16[256,2048]{1,0:T(8,128)(2,1)}, bf16[256,2048]{1,0:T(8,128)(2,1)}, bf16[256,2048]{1,0:T(8,128)(2,1)}, bf16[256,2048]{1,0:T(8,128)(2,1)}) async-done(((bf16[256,2048]{1,0:T(8,128)(2,1)}, bf16[256,2048]{1,0:T(8,128)(2,1)}, bf16[256,2048]{1,0:T(8,128)(2,1)}, bf16[256,2048]{1,0:T(8,128)(2,1)}), (bf16[256,2048]{1,0:T(8,128)(2,1)}, bf16[256,2048]{1,0:T(8,128)(2,1)}, ...) | async-done | bytes 4194320 | tf_op jit(solution)/shard_map/psum | solution.py:15
  397.9 0.0 copy-start.2
  397.9 2.1 fusion.15
  400.1 0.0 copy-done
  400.1 0.0 copy-done.2
  400.1 0.5 fusion.14
  400.6 0.0 copy-start.1
  400.6 0.5 fusion
  401.1 0.7 copy-done.1
  401.8 0.5 fusion.16
  402.3 0.5 fusion.11
  402.8 0.0 copy-start.3
  402.8 0.5 fusion.1
  403.3 0.0 copy-start.6
  403.3 0.7 copy-done.3
  404.0 0.5 fusion.17
  404.5 0.1 copy-done.6
  404.6 0.5 fusion.18
  405.1 0.5 fusion.9
  405.5 2.5 fusion.7
  408.0 0.1 pad_maximum_fusion.36
  408.1 1.6 copy.31
  409.8 0.0 copy-start.5
  409.8 9.9 %all-to-all-start = ((f32[256,4,256]{0,1,2:T(4,128)}), f32[256,4,256]{0,1,2:T(4,128)S(1)}, u32[]{:S(2)}, u32[]{:S(2)}) async-start(f32[256,4,256]{0,1,2:T(4,128)} %copy.31), calls=%async_computation | async-start | bytes 2097152 | tf_op jit(solution)/shard_map/all_to_all | solution.py:75
  419.6 0.0 copy-done.5
  419.6 49.2 %all-gather = s32[1,4096]{1,0:T(1,128)S(1)} all-gather(s32[1,256]{1,0:T(1,128)S(1)} %copy-done.5), channel_id=2, replica_groups=mesh['field'=32,'point'=16] {'point'}, dimensions={1}, use_global_device_ids=true | all-gather | bytes 17408 | tf_op jit(solution)/shard_map/all_gather | solution.py:55
  468.9 0.0 all-to-all-done
  468.9 0.6 copy.32
  469.5 0.6 copy.39
  470.1 2.0 copy.33
  472.1 11.6 %scatter_custom_fusion = f32[64,4096]{0,1:T(8,128)S(1)} fusion(s32[4096]{0:T(1024)S(1)} %compare_select_fusion, f32[4096,64]{1,0:T(8,128)} %copy.33, f32[]{:T(128)} %constant.31.clone.1), kind=kCustom, calls=%fused_computation.88 | custom fusion | bytes 1049088 | tf_op jit(solution)/shard_map/scatter | solution.py:47
  483.7 0.9 copy.38
  484.6 0.1 fusion.45
  484.7 0.2 pad_maximum_fusion
  484.9 0.4 fusion.41
  485.3 2.0 multiply_add_fusion.3
  487.4 0.2 pad_maximum_fusion.1
  487.6 0.4 fusion.40
  488.0 2.0 multiply_add_fusion.2
  490.1 0.2 pad_maximum_fusion.2
  490.3 0.4 fusion.39
  490.7 2.0 multiply_add_fusion.1
  492.8 0.2 pad_maximum_fusion.3
  493.0 0.4 fusion.38
  493.4 2.8 multiply_add_fusion
  (8 shorter events, 0.2 us)
Async XLA Ops:
  6.5 391.4 %all-reduce.3.cloned.1.call-start = ((), (), s32[]{:S(2)}) async-start(), calls=%async_computation.1 | async-start | bytes 8388608 | tf_op jit(solution)/shard_map/psum | solution.py:15
  13.8 1.0 copy-start.4
  15.3 384.8 %copy-start = (bf16[1,256,2048]{2,1,0:T(8,128)(2,1)S(1)}, bf16[1,256,2048]{2,1,0:T(8,128)(2,1)}, u32[]{:S(2)}) copy-start(bf16[1,256,2048]{2,1,0:T(8,128)(2,1)} %param.5) | copy-start | bytes 3145732
  397.9 2.1 copy-start.2
  400.6 1.2 copy-start.1
  402.8 1.2 copy-start.3
  403.3 1.3 copy-start.6
  409.8 9.9 %copy-start.5 = (s32[1,256]{1,0:T(1,128)S(1)}, s32[1,256]{1,0:T(1,128)}, u32[]{:S(2)}) copy-start(s32[1,256]{1,0:T(1,128)} %param.9) | copy-start | bytes 3076
  409.8 59.1 %all-to-all-start = ((f32[256,4,256]{0,1,2:T(4,128)}), f32[256,4,256]{0,1,2:T(4,128)S(1)}, u32[]{:S(2)}, u32[]{:S(2)}) async-start(f32[256,4,256]{0,1,2:T(4,128)} %copy.31), calls=%async_computation | async-start | bytes 2097152 | tf_op jit(solution)/shard_map/all_to_all | solution.py:75
Sparse Core Ops, SparseCore 0:
  14.0 383.9 all-reduce.2
where the time goes:
time: 503 us
  waiting for transfers between devices  383 us (76%)
  blocking collectives  49.2 us (10%)
  local copies, waits for them, and re-layouts  23.6 us (5%)
  between operations  16.2 us (3%)
  other arithmetic  13.1 us (3%)
  starting transfers between devices  9.86 us (2%)
  matrix products  8.38 us (2%)
    psum x1, waiting for transfers between devices, from_root(): return lax.psum(kept, axis)  383 us
    all_gather x1, blocking collectives, per_device(): pixel_ids = lax.all_gather(pixel_of[0], 'point', axis=0, tiled=True)  49.2 us
    scatter x1, local copies, waits for them, and re-layouts, build_maps(): jnp.zeros((count * local_kb, points), jnp.float32).at[:, pixel_ids]  11.6 us
  transfers between devices with their start and end apart: 2, of which 1 were waited for; matrix products, arithmetic and copies ran while one was open for 0% of the time, Pallas kernels for 0%

commit v1 on v0

--- a/solution.py
+++ b/solution.py
@@ -52,7 +52,9 @@
 def per_device(residual_in, coefs_in, dictionary, owner_order, pixel_of):
     residual = residual_in[0]
     coefs = coefs_in[0].astype(jnp.float32)
-    pixel_ids = lax.all_gather(pixel_of[0], "point", axis=0, tiled=True)
+    block = pixel_of[0]
+    sent = jnp.stack([block] * lax.axis_size("point"))
+    pixel_ids = jnp.concatenate(lax.all_to_all(sent, "point", 0, 0), axis=0)
     updated = []
     for turn_index in range(TURNS):
         owner = owner_order[turn_index]

time: 503 us -> 477 us (0.948)
  the two profiles are of different devices: /device:TPU:32 before, /device:TPU:1 now
where the time goes in v1:
time: 477 us
  waiting for transfers between devices  398 us (83%)
  local copies, waits for them, and re-layouts  23.8 us (5%)
  starting transfers between devices  17.8 us (4%)
  between operations  16.2 us (3%)
  other arithmetic  13.1 us (3%)
  matrix products  8.39 us (2%)
    psum x1, waiting for transfers between devices, from_root(): return lax.psum(kept, axis)  371 us
    all_to_all x1, waiting for transfers between devices, per_device(): lax.all_to_all(stacked, 'point', split_axis=2, concat_axis=0, tiled=True)  26.2 us
    scatter x1, local copies, waits for them, and re-layouts, build_maps(): jnp.zeros((count * local_kb, points), jnp.float32).at[:, pixel_ids]  11.6 us
  transfers between devices with their start and end apart: 3, of which 2 were waited for; matrix products, arithmetic and copies ran while one was open for 2% of the time, Pallas kernels for 0%

profile of v1, /device:TPU:1, one launch (start us, length us, event | category | flops | bytes accessed | tf_op | source)
XLA Modules:
  0.0 477.0 jit_solution(15779494919038092413)
XLA Ops:
  6.5 0.0 all-reduce.3.cloned.1.call-start
  6.5 1.5 fusion.46
  10.5 3.3 broadcast_select_fusion.3
  13.8 0.0 copy-start.5
  13.8 0.0 copy-start.4
  13.9 0.0 all-reduce.3.cloned.1.call-update
  13.9 0.7 copy-done.5
  14.5 0.6 stack.18
  15.1 9.2 %all-to-all-start = ((s32[16,1,256]{2,1,0:T(1,128)}), s32[16,1,256]{2,1,0:T(1,128)S(1)}, u32[]{:S(2)}, u32[]{:S(2)}) async-start(s32[16,1,256]{2,1,0:T(1,128)} %stack.18), calls=%async_computation | async-start | bytes 32768 | tf_op jit(solution)/shard_map/all_to_all | solution.py:57
  24.3 0.0 copy-done.4
  24.3 0.3 copy.27
  24.7 0.1 bitcast_convert_fusion
  24.8 0.0 copy-start
  24.8 371.5 %all-reduce.3.cloned.1.call-done = (bf16[256,2048]{1,0:T(8,128)(2,1)}, bf16[256,2048]{1,0:T(8,128)(2,1)}, bf16[256,2048]{1,0:T(8,128)(2,1)}, bf16[256,2048]{1,0:T(8,128)(2,1)}) async-done(((bf16[256,2048]{1,0:T(8,128)(2,1)}, bf16[256,2048]{1,0:T(8,128)(2,1)}, bf16[256,2048]{1,0:T(8,128)(2,1)}, bf16[256,2048]{1,0:T(8,128)(2,1)}), (bf16[256,2048]{1,0:T(8,128)(2,1)}, bf16[256,2048]{1,0:T(8,128)(2,1)}, ...) | async-done | bytes 4194320 | tf_op jit(solution)/shard_map/psum | solution.py:15
  396.3 0.0 copy-start.2
  396.3 2.1 fusion.15
  398.4 0.0 copy-done
  398.4 0.0 copy-done.2
  398.4 0.5 fusion.14
  398.9 0.0 copy-start.1
  398.9 0.5 fusion
  399.4 0.7 copy-done.1
  400.1 0.5 fusion.16
  400.6 0.5 fusion.11
  401.1 0.0 copy-start.3
  401.1 0.5 fusion.1
  401.6 0.0 copy-start.6
  401.6 0.7 copy-done.3
  402.3 0.5 fusion.17
  402.8 0.1 copy-done.6
  402.9 0.5 fusion.18
  403.4 0.5 fusion.9
  403.9 2.5 fusion.7
  406.4 0.1 pad_maximum_fusion.36
  406.4 1.6 copy.31
  408.1 0.0 all-to-all-done
  408.1 8.6 %all-to-all-start.1 = ((f32[256,4,256]{0,1,2:T(4,128)}), f32[256,4,256]{0,1,2:T(4,128)S(1)}, u32[]{:S(2)}, u32[]{:S(2)}) async-start(f32[256,4,256]{0,1,2:T(4,128)} %copy.31), calls=%async_computation.1 | async-start | bytes 2097152 | tf_op jit(solution)/shard_map/all_to_all | solution.py:77
  416.7 26.2 %all-to-all-done.1 = f32[256,4,256]{0,1,2:T(4,128)S(1)} async-done(((f32[256,4,256]{0,1,2:T(4,128)}), f32[256,4,256]{0,1,2:T(4,128)S(1)}, u32[]{:S(2)}, u32[]{:S(2)}) %all-to-all-start.1) | async-done | bytes 1048608 | tf_op jit(solution)/shard_map/all_to_all | solution.py:77
  442.9 0.6 copy.32
  443.5 0.6 copy.39
  444.1 1.9 copy.33
  446.1 11.6 %scatter_custom_fusion = f32[64,4096]{0,1:T(8,128)S(1)} fusion(s32[4096]{0:T(1024)S(1)} %bitcast.85, f32[4096,64]{1,0:T(8,128)} %copy.33, f32[]{:T(128)} %constant.31.clone.1), kind=kCustom, calls=%fused_computation.88 | custom fusion | bytes 1049088 | tf_op jit(solution)/shard_map/scatter | solution.py:47
  457.7 0.9 copy.38
  458.6 0.1 fusion.45
  458.7 0.2 pad_maximum_fusion
  458.9 0.4 fusion.41
  459.3 2.0 multiply_add_fusion.3
  461.4 0.2 pad_maximum_fusion.1
  461.6 0.4 fusion.40
  462.0 2.0 multiply_add_fusion.2
  464.1 0.2 pad_maximum_fusion.2
  464.3 0.4 fusion.39
  464.7 2.0 multiply_add_fusion.1
  466.8 0.2 pad_maximum_fusion.3
  467.0 0.4 fusion.38
  467.4 2.8 multiply_add_fusion
  (8 shorter events, 0.2 us)
Async XLA Ops:
  6.5 389.7 %all-reduce.3.cloned.1.call-start = ((), (), s32[]{:S(2)}) async-start(), calls=%async_computation.2 | async-start | bytes 8388608 | tf_op jit(solution)/shard_map/psum | solution.py:15
  13.8 0.7 copy-start.5
  13.8 10.5 %copy-start.4 = (bf16[1,256,4,256]{3,2,1,0:T(4,128)(2,1)S(1)}, bf16[1,256,4,256]{3,2,1,0:T(4,128)(2,1)}, u32[]{:S(2)}) copy-start(bf16[1,256,4,256]{3,2,1,0:T(4,128)(2,1)} %param.6) | copy-start | bytes 1572868
  15.1 393.0 %all-to-all-start = ((s32[16,1,256]{2,1,0:T(1,128)}), s32[16,1,256]{2,1,0:T(1,128)S(1)}, u32[]{:S(2)}, u32[]{:S(2)}) async-start(s32[16,1,256]{2,1,0:T(1,128)} %stack.18), calls=%async_computation | async-start | bytes 32768 | tf_op jit(solution)/shard_map/all_to_all | solution.py:57
  24.8 373.6 %copy-start = (bf16[1,256,2048]{2,1,0:T(8,128)(2,1)S(1)}, bf16[1,256,2048]{2,1,0:T(8,128)(2,1)}, u32[]{:S(2)}) copy-start(bf16[1,256,2048]{2,1,0:T(8,128)(2,1)} %param.5) | copy-start | bytes 3145732
  396.3 2.1 copy-start.2
  398.9 1.2 copy-start.1
  401.1 1.2 copy-start.3
  401.6 1.3 copy-start.6
  408.1 34.8 %all-to-all-start.1 = ((f32[256,4,256]{0,1,2:T(4,128)}), f32[256,4,256]{0,1,2:T(4,128)S(1)}, u32[]{:S(2)}, u32[]{:S(2)}) async-start(f32[256,4,256]{0,1,2:T(4,128)} %copy.31), calls=%async_computation.1 | async-start | bytes 2097152 | tf_op jit(solution)/shard_map/all_to_all | solution.py:77
Sparse Core Ops, SparseCore 0:
  14.0 382.2 all-reduce.2
